TPU v7x, 32 devices: a whole 2x2x4 slice. The times are simulated.
32 devices in a mesh: tm: 8 (over z, y), emit: 4 (over x, core).
Axes of the slice: x: 2, y: 2, z: 4, core: 2. Of those that a mesh axis runs over, the one named last changes fastest.
Arguments:
- observed: int32 [8, 512], P('emit', 'tm'), may hold values from 0 to 4095
- starts: int32 [8], P('emit'), may hold values from 0 to 255
- initial: float32 [256], replicated, may hold values from 0.1 to 1
- transition: float32 [256, 256], replicated, may hold values from 0 to 1, as said below
- emission: float32 [4096, 256], P('emit'), may hold values from 0.5 to 2
Outputs:
- posterior: float32 [8, 512, 256], P('emit', 'tm')
- new_emission: float32 [4096, 256], P(('tm', 'emit'))
- loglik: float32 [8], P('emit')
Inputs may be any that keep to these rules, and one draw needn't show every extreme that they name: `transition`: entries positive.
All inputs are finite; a program needn't handle non-finite values.
Results may differ from a plain program's by a relative error of at most 0.0003.
Values sent between devices are 32-bit elements; how exact they have to be, the bound alone decides.
No kernel may reach another device: no remote copies, remote signals or barrier semaphores. Data moves between devices by JAX's collectives and lax.ppermute only.
A program may use at most 128 MiB of HBM per device.

v0:
```python
import jax
import jax.numpy as jnp
from jax import lax
from jax.sharding import PartitionSpec as P

highest = lax.Precision.HIGHEST
pseudo_count = 0.01


def from_behind(value, axis, by):
    peers = lax.axis_size(axis)
    pairs = [(i, i + by) for i in range(peers) if 0 <= i + by < peers]
    return lax.ppermute(value, axis, pairs)


def normalize_rows(values):
    return values / jnp.sum(values, axis=-1, keepdims=True)


def normalize_blocks(matrices):
    return matrices / jnp.sum(matrices, axis=(1, 2), keepdims=True)


def shards(observed, starts, initial, transition, emission):
    traj_rows, frame_count = observed.shape
    states = transition.shape[0]
    tm_count = lax.axis_size("tm")
    tm_place = lax.axis_index("tm")
    emit_count = lax.axis_size("emit")
    own_rows = emission.shape[0]
    total_rows = own_rows * emit_count
    positions = tm_place * frame_count + jnp.arange(frame_count, dtype=jnp.int32)
    active = positions[None, :] >= starts[:, None]
    block_rows = lax.all_gather(emission, "emit", axis=0, tiled=True)
    local_ids = observed
    inside = (local_ids >= 0) & (local_ids < block_rows.shape[0])
    taken = jnp.take(block_rows, jnp.clip(local_ids, 0, block_rows.shape[0] - 1), axis=0)
    weights = jnp.where(inside[:, :, None], taken, 0.0)
    weight_seq = jnp.swapaxes(weights, 0, 1)
    active_seq = active.T
    eye_block = jnp.broadcast_to(jnp.eye(states, dtype=jnp.float32), (traj_rows, states, states))

    def product_step(carried, inputs):
        weight_now, active_now = inputs
        moved = (
            jnp.einsum("nij,jk->nik", carried, transition, precision=highest)
            * weight_now[:, None, :]
        )
        moved = normalize_blocks(moved)
        return (jnp.where(active_now[:, None, None], moved, carried), None)

    transfer, _ = lax.scan(product_step, eye_block, (weight_seq, active_seq))
    prior_state = jnp.broadcast_to(initial / jnp.sum(initial), (traj_rows, states))
    final_state = jnp.full((traj_rows, states), 1.0 / states, jnp.float32)

    def relay_round(round_index, carried):
        forward_in, backward_in = carried
        forward_out = normalize_rows(
            jnp.einsum("ni,nij->nj", forward_in, transfer, precision=highest)
        )
        backward_out = normalize_rows(
            jnp.einsum("nij,nj->ni", transfer, backward_in, precision=highest)
        )
        from_left = from_behind(forward_out, "tm", 1)
        from_right = from_behind(backward_out, "tm", -1)
        forward_in = jnp.where(tm_place == 0, prior_state, from_left)
        backward_in = jnp.where(tm_place == tm_count - 1, final_state, from_right)
        return (forward_in, backward_in)

    forward_in, backward_in = lax.fori_loop(
        0, tm_count - 1, relay_round, (prior_state, final_state)
    )

    def forward_step(previous, inputs):
        weight_now, active_now = inputs
        moved = jnp.dot(previous, transition, precision=highest) * weight_now
        scaling = jnp.sum(moved, axis=1)
        updated = jnp.where(active_now[:, None], moved / scaling[:, None], previous)
        return (updated, (updated, jnp.where(active_now, jnp.log(scaling), 0.0)))

    _, (forward, log_scales) = lax.scan(forward_step, forward_in, (weight_seq, active_seq))

    def backward_step(later_msg, inputs):
        weight_now, active_now = inputs
        moved = jnp.dot(later_msg * weight_now, transition.T, precision=highest)
        earlier = jnp.where(active_now[:, None], normalize_rows(moved), later_msg)
        return (earlier, later_msg)

    _, backward = lax.scan(backward_step, backward_in, (weight_seq, active_seq), reverse=True)
    joint_prob = forward * backward
    occupancy = jnp.where(active_seq[:, :, None], normalize_rows(joint_prob), 0.0)
    posterior = jnp.swapaxes(states * occupancy, 0, 1)
    loglik_local = jnp.sum(log_scales, axis=0)
    occ_rows = jnp.swapaxes(occupancy, 0, 1).reshape(-1, states)
    frame_list = observed.reshape(-1)
    block = total_rows // (tm_count * emit_count)
    local_ids = frame_list
    inside = (local_ids >= 0) & (local_ids < block * lax.axis_size(("tm", "emit")))
    counts = lax.psum_scatter(
        jax.ops.segment_sum(
            jnp.where(inside[:, None], occ_rows, 0.0),
            jnp.clip(local_ids, 0, block * lax.axis_size(("tm", "emit")) - 1),
            num_segments=block * lax.axis_size(("tm", "emit")),
        ),
        ("tm", "emit"),
        scatter_dimension=0,
        tiled=True,
    )
    totals = lax.psum(jnp.sum(counts, axis=0), ("tm", "emit"))
    loglik_sum = lax.psum(loglik_local, "tm")
    new_emission = total_rows * (counts + pseudo_count) / (totals + total_rows * pseudo_count)
    loglik = loglik_sum / (frame_count * tm_count - starts).astype(jnp.float32)
    return (posterior, new_emission, loglik)


def solution(mesh):
    in_specs = (P("emit", "tm"), P("emit"), P(), P(), P("emit", None))
    out_specs = (P("emit", "tm", None), P(("tm", "emit"), None), P("emit"))
    return jax.shard_map(shards, mesh=mesh, in_specs=in_specs, out_specs=out_specs, check_vma=False)
```

profile of v0, /device:TPU:10, one launch (start us, length us, event | category | flops | bytes accessed | tf_op | source)
XLA Modules:
  0.0 506.8 jit_solution(13056474050517089215)
XLA Ops:
  13.1 31.2 %all-gather.2.cloned.1.call-done = f32[4096,256]{1,0:T(8,128)} async-done(((f32[1024,256]{1,0:T(8,128)}), f32[4096,256]{1,0:T(8,128)}) %all-gather.2.cloned.1.call-update) | async-done | bytes 4194320 | tf_op jit(solution)/shard_map/all_gather | solution.py:34
  44.2 2.9 gather_fusion
  47.4 117.4 %while.55 = (s32[]{:T(128)}, f32[2,256,256]{2,1,0:T(8,128)S(1)}, pred[64,2]{1,0:T(8,128)(4,1)S(1)}, f32[256,256]{1,0:T(8,128)}, f32[64,2,256]{2,1,0:T(2,128)S(1)}, /*index=5*/s32[]{:T(128)}) while((s32[]{:T(128)}, f32[2,256,256]{2,1,0:T(8,128)S(1)}, pred[64,2]{1,0:T(8,128)(4,1)S(1)}, f32[256,256]{1,0:T(8,128)}, f32[64,2,256]{2,1,0:T(2,128)S(1)}, ...), condition=%wide.region_3.4_spmd, body=%wide.region_1.3_spmd.sunk | while | flops 403177472 | bytes 2889835 | solution.py:52
  47.5 1.6 fusion.42
  53.0 1.6 fusion.42
  54.8 1.6 fusion.42
  56.7 1.6 fusion.42
  58.5 1.6 fusion.42
  62.2 1.6 fusion.42
  64.0 1.6 fusion.42
  65.8 1.6 fusion.42
  67.7 1.6 fusion.42
  71.3 1.6 fusion.42
  73.2 1.6 fusion.42
  75.0 1.6 fusion.42
  76.8 1.6 fusion.42
  80.5 1.6 fusion.42
  82.3 1.6 fusion.42
  84.2 1.6 fusion.42
  86.0 1.6 fusion.42
  89.7 1.6 fusion.42
  91.5 1.6 fusion.42
  93.3 1.6 fusion.42
  95.2 1.6 fusion.42
  98.9 1.6 fusion.42
  100.7 1.6 fusion.42
  102.5 1.6 fusion.42
  104.4 1.6 fusion.42
  109.9 1.6 fusion.42
  111.7 1.6 fusion.42
  113.5 1.6 fusion.42
  120.9 1.6 fusion.42
  130.0 1.6 fusion.42
  139.2 1.6 fusion.42
  148.4 1.6 fusion.42
  157.5 1.6 fusion.42
  164.9 68.8 %while.58 = (s32[]{:T(128)}, f32[2,256]{1,0:T(2,128)S(1)}, f32[2,256]{1,0:T(2,128)S(1)}, pred[]{:T(512)}, f32[2,256,256]{2,1,0:T(8,128)S(1)}, /*index=5*/pred[]{:T(512)}, f32[256]{0:T(256)S(1)}, s32[]{:T(128)}, s32[]{:T(128)}) while((s32[]{:T(128)}, f32[2,256]{1,0:T(2,128)S(1)}, f32[2,256]{1,0:T(2,128)S(1)}, pred[]{:T(512)}, ...), condition=%wide.region_7.8_spmd.clone, body=%wide.region_4.7_spmd.clone.sunk | while | flops 3149311 | bytes 1098969 | solution.py:70
  165.6 3.4 collective-permute-start.1
  169.6 2.5 collective-permute-start
  172.1 3.9 collective-permute-done
  176.7 1.9 collective-permute-start.1
  179.2 3.9 collective-permute-start
  183.1 2.4 collective-permute-done
  186.3 1.9 collective-permute-start.1
  188.8 3.9 collective-permute-start
  192.7 2.4 collective-permute-done
  195.9 1.9 collective-permute-start.1
  198.4 3.9 collective-permute-start
  202.4 2.4 collective-permute-done
  205.5 1.9 collective-permute-start.1
  208.0 3.9 collective-permute-start
  212.0 2.4 collective-permute-done
  215.2 1.9 collective-permute-start.1
  217.6 3.9 collective-permute-start
  221.6 2.4 collective-permute-done
  224.8 1.9 collective-permute-start.1
  227.3 3.9 collective-permute-start
  231.2 2.4 collective-permute-done
  233.7 38.5 %while.57 = (s32[]{:T(128)}, f32[2,256]{1,0:T(2,128)S(1)}, f32[64,2,256]{2,0,1:T(8,128)S(1)}, pred[64,2]{1,0:T(8,128)(4,1)S(1)}, f32[64,2,256]{2,1,0:T(2,128)S(1...) while((s32[]{:T(128)}, f32[2,256]{1,0:T(2,128)S(1)}, f32[64,2,256]{2,0,1:T(8,128)S(1)}, ...), condition=%wide.region_13.14_spmd, body=%wide.region_11.13_spmd.sunk | while | flops 1574913 | bytes 282763 | solution.py:89
  272.2 36.6 %while.56 = (s32[]{:T(128)}, f32[2,256]{1,0:T(2,128)S(1)}, f32[64,2,256]{2,0,1:T(8,128)S(1)}, f32[64,2]{1,0:T(8,128)S(1)}, pred[64,2]{1,0:T(8,128)(4,1)S(1)}, /*...) while((s32[]{:T(128)}, f32[2,256]{1,0:T(2,128)S(1)}, ...), condition=%wide.region_10.11_spmd, body=%wide.region_8.10_spmd.sunk | while | flops 1574914 | bytes 282801 | solution.py:81
  309.3 3.4 scatter_custom_fusion
  312.7 20.5 %psum.15 = f32[2]{0:T(128)S(1)} all-reduce(f32[2]{0:T(128)S(1)} %reduce_sum.94), channel_id=1, replica_groups=mesh['tm'=8,'emit'=4] {'tm'}, use_global_device_ids=true, to_apply=%region_20.21 | all-reduce | flops 2 | bytes 16 | tf_op jit(solution)/shard_map/psum | solution.py:110
  334.4 99.9 %reduce-scatter.2.cloned.1.call-done = f32[128,256]{1,0:T(8,128)} async-done(((f32[4096,256]{1,0:T(8,128)}), f32[128,256]{1,0:T(8,128)}) %reduce-scatter.2.cloned.1.call-update) | async-done | bytes 131088 | tf_op jit(solution)/shard_map/reduce_scatter | solution.py:99
  435.3 63.1 %psum.14 = f32[256]{0:T(256)S(1)} all-reduce(f32[256]{0:T(256)S(1)} %reduce_sum.93), channel_id=1, replica_groups=mesh['tm'=8,'emit'=4] {'tm','emit'}, use_global_device_ids=true, to_apply=%region_18.19 | all-reduce | flops 256 | bytes 2048 | tf_op jit(solution)/shard_map/psum | solution.py:109
  (1097 shorter events, 150.2 us)
Async XLA Ops:
  7.2 37.1 %all-gather.2.cloned.1.call-start = ((), (), s32[]{:S(2)}) async-start(), calls=%async_computation.1 | async-start | bytes 5242880 | tf_op jit(solution)/shard_map/all_gather | solution.py:34
  7.9 426.4 %reduce-scatter.2.cloned.1.call-start = ((), (), s32[]{:S(2)}) async-start(), calls=%async_computation.2 | async-start | bytes 4325376 | tf_op jit(solution)/shard_map/reduce_scatter | solution.py:99
  164.8 68.8 %copy-start = (f32[256,256]{1,0:T(8,128)S(1)}, f32[256,256]{1,0:T(8,128)}, u32[]{:S(2)}) copy-start(f32[256,256]{1,0:T(8,128)} %get-tuple-element.664) | copy-start | bytes 786436
  165.6 6.4 %collective-permute-start.1 = (f32[2,256]{1,0:T(2,128)S(1)}, f32[2,256]{1,0:T(2,128)S(1)}, u32[]{:S(2)}, u32[]{:S(2)}) collective-permute-start(f32[2,256]{1,0:T(2,128)S(1)} %bitcast_divide_fusion.5), channel_id=1, source_target_pairs={{4,0},{8,4},{12,8},{16,12},{20,16},{24,20},{28,24},{5,1},{9,5},{13... | collective-permute-start | bytes 6152 | tf_op jit(solution)/shard_map/while/body/eval_jaxpr/ppermute | solution.py:13
  169.6 6.4 %collective-permute-start = (f32[2,256]{1,0:T(2,128)S(1)}, f32[2,256]{1,0:T(2,128)S(1)}, u32[]{:S(2)}, u32[]{:S(2)}) collective-permute-start(f32[2,256]{1,0:T(2,128)S(1)} %bitcast_divide_fusion.4), channel_id=1, source_target_pairs={{0,4},{4,8},{8,12},{12,16},{16,20},{20,24},{24,28},{1,5},{5,9},{9,... | collective-permute-start | bytes 6152 | tf_op jit(solution)/shard_map/while/body/eval_jaxpr/ppermute | solution.py:13
  176.7 6.4 %collective-permute-start.1 = (f32[2,256]{1,0:T(2,128)S(1)}, f32[2,256]{1,0:T(2,128)S(1)}, u32[]{:S(2)}, u32[]{:S(2)}) collective-permute-start(f32[2,256]{1,0:T(2,128)S(1)} %bitcast_divide_fusion.5), channel_id=1, source_target_pairs={{4,0},{8,4},{12,8},{16,12},{20,16},{24,20},{28,24},{5,1},{9,5},{13... | collective-permute-start | bytes 6152 | tf_op jit(solution)/shard_map/while/body/eval_jaxpr/ppermute | solution.py:13
  179.2 6.4 %collective-permute-start = (f32[2,256]{1,0:T(2,128)S(1)}, f32[2,256]{1,0:T(2,128)S(1)}, u32[]{:S(2)}, u32[]{:S(2)}) collective-permute-start(f32[2,256]{1,0:T(2,128)S(1)} %bitcast_divide_fusion.4), channel_id=1, source_target_pairs={{0,4},{4,8},{8,12},{12,16},{16,20},{20,24},{24,28},{1,5},{5,9},{9,... | collective-permute-start | bytes 6152 | tf_op jit(solution)/shard_map/while/body/eval_jaxpr/ppermute | solution.py:13
  186.3 6.4 %collective-permute-start.1 = (f32[2,256]{1,0:T(2,128)S(1)}, f32[2,256]{1,0:T(2,128)S(1)}, u32[]{:S(2)}, u32[]{:S(2)}) collective-permute-start(f32[2,256]{1,0:T(2,128)S(1)} %bitcast_divide_fusion.5), channel_id=1, source_target_pairs={{4,0},{8,4},{12,8},{16,12},{20,16},{24,20},{28,24},{5,1},{9,5},{13... | collective-permute-start | bytes 6152 | tf_op jit(solution)/shard_map/while/body/eval_jaxpr/ppermute | solution.py:13
  188.8 6.4 %collective-permute-start = (f32[2,256]{1,0:T(2,128)S(1)}, f32[2,256]{1,0:T(2,128)S(1)}, u32[]{:S(2)}, u32[]{:S(2)}) collective-permute-start(f32[2,256]{1,0:T(2,128)S(1)} %bitcast_divide_fusion.4), channel_id=1, source_target_pairs={{0,4},{4,8},{8,12},{12,16},{16,20},{20,24},{24,28},{1,5},{5,9},{9,... | collective-permute-start | bytes 6152 | tf_op jit(solution)/shard_map/while/body/eval_jaxpr/ppermute | solution.py:13
  195.9 6.4 %collective-permute-start.1 = (f32[2,256]{1,0:T(2,128)S(1)}, f32[2,256]{1,0:T(2,128)S(1)}, u32[]{:S(2)}, u32[]{:S(2)}) collective-permute-start(f32[2,256]{1,0:T(2,128)S(1)} %bitcast_divide_fusion.5), channel_id=1, source_target_pairs={{4,0},{8,4},{12,8},{16,12},{20,16},{24,20},{28,24},{5,1},{9,5},{13... | collective-permute-start | bytes 6152 | tf_op jit(solution)/shard_map/while/body/eval_jaxpr/ppermute | solution.py:13
  198.4 6.4 %collective-permute-start = (f32[2,256]{1,0:T(2,128)S(1)}, f32[2,256]{1,0:T(2,128)S(1)}, u32[]{:S(2)}, u32[]{:S(2)}) collective-permute-start(f32[2,256]{1,0:T(2,128)S(1)} %bitcast_divide_fusion.4), channel_id=1, source_target_pairs={{0,4},{4,8},{8,12},{12,16},{16,20},{20,24},{24,28},{1,5},{5,9},{9,... | collective-permute-start | bytes 6152 | tf_op jit(solution)/shard_map/while/body/eval_jaxpr/ppermute | solution.py:13
  205.5 6.4 %collective-permute-start.1 = (f32[2,256]{1,0:T(2,128)S(1)}, f32[2,256]{1,0:T(2,128)S(1)}, u32[]{:S(2)}, u32[]{:S(2)}) collective-permute-start(f32[2,256]{1,0:T(2,128)S(1)} %bitcast_divide_fusion.5), channel_id=1, source_target_pairs={{4,0},{8,4},{12,8},{16,12},{20,16},{24,20},{28,24},{5,1},{9,5},{13... | collective-permute-start | bytes 6152 | tf_op jit(solution)/shard_map/while/body/eval_jaxpr/ppermute | solution.py:13
  208.0 6.4 %collective-permute-start = (f32[2,256]{1,0:T(2,128)S(1)}, f32[2,256]{1,0:T(2,128)S(1)}, u32[]{:S(2)}, u32[]{:S(2)}) collective-permute-start(f32[2,256]{1,0:T(2,128)S(1)} %bitcast_divide_fusion.4), channel_id=1, source_target_pairs={{0,4},{4,8},{8,12},{12,16},{16,20},{20,24},{24,28},{1,5},{5,9},{9,... | collective-permute-start | bytes 6152 | tf_op jit(solution)/shard_map/while/body/eval_jaxpr/ppermute | solution.py:13
  215.2 6.4 %collective-permute-start.1 = (f32[2,256]{1,0:T(2,128)S(1)}, f32[2,256]{1,0:T(2,128)S(1)}, u32[]{:S(2)}, u32[]{:S(2)}) collective-permute-start(f32[2,256]{1,0:T(2,128)S(1)} %bitcast_divide_fusion.5), channel_id=1, source_target_pairs={{4,0},{8,4},{12,8},{16,12},{20,16},{24,20},{28,24},{5,1},{9,5},{13... | collective-permute-start | bytes 6152 | tf_op jit(solution)/shard_map/while/body/eval_jaxpr/ppermute | solution.py:13
  217.6 6.4 %collective-permute-start = (f32[2,256]{1,0:T(2,128)S(1)}, f32[2,256]{1,0:T(2,128)S(1)}, u32[]{:S(2)}, u32[]{:S(2)}) collective-permute-start(f32[2,256]{1,0:T(2,128)S(1)} %bitcast_divide_fusion.4), channel_id=1, source_target_pairs={{0,4},{4,8},{8,12},{12,16},{16,20},{20,24},{24,28},{1,5},{5,9},{9,... | collective-permute-start | bytes 6152 | tf_op jit(solution)/shard_map/while/body/eval_jaxpr/ppermute | solution.py:13
  224.8 6.4 %collective-permute-start.1 = (f32[2,256]{1,0:T(2,128)S(1)}, f32[2,256]{1,0:T(2,128)S(1)}, u32[]{:S(2)}, u32[]{:S(2)}) collective-permute-start(f32[2,256]{1,0:T(2,128)S(1)} %bitcast_divide_fusion.5), channel_id=1, source_target_pairs={{4,0},{8,4},{12,8},{16,12},{20,16},{24,20},{28,24},{5,1},{9,5},{13... | collective-permute-start | bytes 6152 | tf_op jit(solution)/shard_map/while/body/eval_jaxpr/ppermute | solution.py:13
  227.3 6.4 %collective-permute-start = (f32[2,256]{1,0:T(2,128)S(1)}, f32[2,256]{1,0:T(2,128)S(1)}, u32[]{:S(2)}, u32[]{:S(2)}) collective-permute-start(f32[2,256]{1,0:T(2,128)S(1)} %bitcast_divide_fusion.4), channel_id=1, source_target_pairs={{0,4},{4,8},{8,12},{12,16},{16,20},{20,24},{24,28},{1,5},{5,9},{9,... | collective-permute-start | bytes 6152 | tf_op jit(solution)/shard_map/while/body/eval_jaxpr/ppermute | solution.py:13
  309.3 24.0 %copy-start.1 = (s32[2]{0:T(128)S(1)}, s32[2]{0:T(128)}, u32[]{:S(2)}) copy-start(s32[2]{0:T(128)} %param.14) | copy-start | bytes 28
Sparse Core Ops, SparseCore 0:
  9.5 34.6 all-gather.1
  312.8 121.4 reduce-scatter.1
where the time goes:
time: 510 us; the launch traced here: 507 us
  matrix products  159 us (31%)
  waiting for transfers between devices  150 us (29%)
  blocking collectives  83.6 us (16%)
  starting transfers between devices  41 us (8%)
  other arithmetic  36.2 us (7%)
  local copies, waits for them, and re-layouts  14.3 us (3%)
  between operations  14.2 us (3%)
  loops' own time  8.47 us (2%)
    dot_general x64, matrix products, product_step(): jnp.einsum('nij,jk->nik', carried, transition, precision=highest)  104 us
    reduce_scatter x1, waiting for transfers between devices, shards(): lax.psum_scatter(jax.ops.segment_sum(jnp.where(inside[:, None], occ_rows,...  99.9 us
    psum x1, blocking collectives, shards(): totals = lax.psum(jnp.sum(counts, axis=0), ('tm', 'emit'))  63.1 us
    ppermute x14, starting transfers between devices, from_behind(): return lax.ppermute(value, axis, pairs)  40.9 us
    all_gather x1, waiting for transfers between devices, shards(): block_rows = lax.all_gather(emission, 'emit', axis=0, tiled=True)  31.2 us
    dot_general x64, matrix products, backward_step(): moved = jnp.dot(later_msg * weight_now, transition.T, precision=highest)  27.4 us
    dot_general x64, matrix products, forward_step(): moved = jnp.dot(previous, transition, precision=highest) * weight_now  21.3 us
    psum x1, blocking collectives, shards(): loglik_sum = lax.psum(loglik_local, 'tm')  20.5 us
  transfers between devices with their start and end apart: 16, of which 9 were waited for; matrix products, arithmetic and copies ran while one was open for 2% of the time, Pallas kernels for 0%

commit v1 on v0

--- a/solution.py
+++ b/solution.py
@@ -31,7 +31,22 @@
     total_rows = own_rows * emit_count
     positions = tm_place * frame_count + jnp.arange(frame_count, dtype=jnp.int32)
     active = positions[None, :] >= starts[:, None]
-    block_rows = lax.all_gather(emission, "emit", axis=0, tiled=True)
+    x_local = emission
+    w2, current_value, formed = (lax.psum(1, "emit"), lax.axis_index("emit"), x_local.shape[0])
+    row_list = []
+    for tick, dd in enumerate(x_local.shape):
+        row_list.append(dd * w2 if tick == 0 else dd)
+    block_rows = lax.dynamic_update_slice_in_dim(
+        jnp.zeros(row_list, x_local.dtype), x_local, current_value * formed, axis=0
+    )
+    for c in range(1, w2):
+        series = []
+        for tick in range(w2):
+            series.append((tick, (tick + 1) % w2))
+        x_local = lax.ppermute(x_local, axis_name="emit", perm=series)
+        block_rows = lax.dynamic_update_slice_in_dim(
+            block_rows, x_local, (current_value - c) % w2 * formed, axis=0
+        )
     local_ids = observed
     inside = (local_ids >= 0) & (local_ids < block_rows.shape[0])
     taken = jnp.take(block_rows, jnp.clip(local_ids, 0, block_rows.shape[0] - 1), axis=0)

time: 510 us -> 453 us (0.89)
  matrix products: 159 us -> 97.8 us
  local copies, waits for them, and re-layouts: 14.3 us -> 20.6 us
    dot_general x64, matrix products: 104 us -> 43.1 us  [product_step(): jnp.einsum('nij,jk->nik', carried, transition, precision=highest)]
    ppermute x0 -> x3, waiting for transfers between devices: none -> 33.1 us  [shards(): x_local = lax.ppermute(x_local, axis_name='emit', perm=series)]
    all_gather x1 -> x0, waiting for transfers between devices: 31.2 us -> none  [shards(): block_rows = lax.all_gather(emission, 'emit', axis=0, tiled=True)]
    dynamic_update_slice x0 -> x4, local copies, waits for them, and re-layouts: none -> 5.49 us  [the longest x3 4.44 us: shards(): lax.dynamic_update_slice_in_dim(block_rows, x_local, (current_value - c)...]
  transfers between devices with their start and end apart: 16 -> 18, of which waited for: 9 -> 11; matrix products, arithmetic and copies ran while one was open for 2% -> 3% of each run, Pallas kernels for 0% -> 0%
where the time goes in v1:
time: 453 us; the launch traced here: 452 us
  waiting for transfers between devices  152 us (34%)
  matrix products  97.8 us (22%)
  blocking collectives  83.6 us (18%)
  starting transfers between devices  41 us (9%)
  other arithmetic  35.7 us (8%)
  local copies, waits for them, and re-layouts  20.6 us (5%)
  between operations  14.2 us (3%)
  loops' own time  7.32 us (2%)
    reduce_scatter x1, waiting for transfers between devices, shards(): lax.psum_scatter(jax.ops.segment_sum(jnp.where(inside[:, None], occ_rows,...  100 us
    psum x1, blocking collectives, shards(): totals = lax.psum(jnp.sum(counts, axis=0), ('tm', 'emit'))  63.2 us
    dot_general x64, matrix products, product_step(): jnp.einsum('nij,jk->nik', carried, transition, precision=highest)  43.1 us
    ppermute x14, starting transfers between devices, from_behind(): return lax.ppermute(value, axis, pairs)  40.9 us
    ppermute x3, waiting for transfers between devices, shards(): x_local = lax.ppermute(x_local, axis_name='emit', perm=series)  33.1 us
    dot_general x64, matrix products, backward_step(): moved = jnp.dot(later_msg * weight_now, transition.T, precision=highest)  27.2 us
    dot_general x64, matrix products, forward_step(): moved = jnp.dot(previous, transition, precision=highest) * weight_now  21.2 us
    psum x1, blocking collectives, shards(): loglik_sum = lax.psum(loglik_local, 'tm')  20.5 us
  transfers between devices with their start and end apart: 18, of which 11 were waited for; matrix products, arithmetic and copies ran while one was open for 3% of the time, Pallas kernels for 0%

profile of v1, /device:TPU:10, one launch (start us, length us, event | category | flops | bytes accessed | tf_op | source)
XLA Modules:
  0.0 451.9 jit_solution(13030395742426601448)
XLA Ops:
  7.3 14.4 %collective-permute-done.2 = f32[1024,256]{1,0:T(8,128)S(1)} collective-permute-done((f32[1024,256]{1,0:T(8,128)}, f32[1024,256]{1,0:T(8,128)S(1)}, u32[]{:S(2)}, u32[]{:S(2)}) %collective-permute-start.2) | collective-permute-done | bytes 1048608 | tf_op jit(solution)/shard_map/ppermute | solution.py:46
  21.7 0.7 broadcast_clamp_fusion
  22.5 0.7 broadcast_compare_fusion
  23.3 12.6 %collective-permute-done.3 = f32[1024,256]{1,0:T(8,128)S(1)} collective-permute-done((f32[1024,256]{1,0:T(8,128)S(1)}, f32[1024,256]{1,0:T(8,128)S(1)}, u32[]{:S(2)}, u32[]{:S(2)}) %collective-permute-start.3) | collective-permute-done | bytes 1048608 | tf_op jit(solution)/shard_map/ppermute | solution.py:46
  35.9 0.7 compare_and_fusion
  36.8 1.3 reduce_sum.91
  38.1 2.2 broadcast.78
  40.3 1.1 constant_dynamic-update-slice_fusion.3
  42.0 1.1 constant_dynamic-update-slice_fusion.2
  43.1 1.1 constant_dynamic-update-slice_fusion.1
  44.2 6.1 %collective-permute-done.4 = f32[1024,256]{1,0:T(8,128)} collective-permute-done((f32[1024,256]{1,0:T(8,128)S(1)}, f32[1024,256]{1,0:T(8,128)}, u32[]{:S(2)}, u32[]{:S(2)}) %collective-permute-start.4) | collective-permute-done | bytes 1048608 | tf_op jit(solution)/shard_map/ppermute | solution.py:46
  50.3 2.3 constant_dynamic-update-slice_fusion
  52.5 2.9 gather_fusion
  55.8 56.0 %while.55 = (s32[]{:T(128)}, f32[2,256,256]{2,1,0:T(8,128)S(1)}, pred[64,2]{1,0:T(8,128)(4,1)S(1)}, f32[256,256]{1,0:T(8,128)S(1)}, f32[64,2,256]{2,1,0:T(2,128)S(1)}, /*index=5*/s32[]{:T(128)}) while((s32[]{:T(128)}, f32[2,256,256]{2,1,0:T(8,128)S(1)}, pred[64,2]{1,0:T(8,128)(4,1)S(1)}, f32[256,256]{1,0:T(8,128)S(1)}, ...), condition=%wide.region_3.4_spmd, body=%wide.region_1.3_spmd.sunk | while | flops 403177472 | bytes 2889827 | solution.py:67
  56.7 0.7 fusion.42
  60.2 0.7 fusion.42
  61.0 0.7 fusion.42
  63.7 0.7 fusion.42
  64.5 0.7 fusion.42
  67.2 0.7 fusion.42
  68.0 0.7 fusion.42
  70.7 0.7 fusion.42
  74.2 0.7 fusion.42
  77.7 0.7 fusion.42
  81.2 0.7 fusion.42
  84.7 0.7 fusion.42
  88.2 0.7 fusion.42
  91.7 0.7 fusion.42
  95.2 0.7 fusion.42
  98.7 0.7 fusion.42
  99.6 0.7 fusion.42
  102.2 0.7 fusion.42
  105.7 0.7 fusion.42
  109.2 0.7 fusion.42
  111.8 68.7 %while.58 = (s32[]{:T(128)}, f32[2,256]{1,0:T(2,128)S(1)}, f32[2,256]{1,0:T(2,128)S(1)}, pred[]{:T(512)}, f32[2,256,256]{2,1,0:T(8,128)S(1)}, /*index=5*/pred[]{:T(512)}, f32[256]{0:T(256)S(1)}, s32[]{:T(128)}, s32[]{:T(128)}) while((s32[]{:T(128)}, f32[2,256]{1,0:T(2,128)S(1)}, f32[2,256]{1,0:T(2,128)S(1)}, pred[]{:T(512)}, ...), condition=%wide.region_7.8_spmd.clone, body=%wide.region_4.7_spmd.clone.sunk | while | flops 3149311 | bytes 1098969 | solution.py:85
  112.6 3.3 collective-permute-start.1
  116.5 2.5 collective-permute-start
  119.0 3.8 collective-permute-done
  123.6 1.9 collective-permute-start.1
  126.1 3.9 collective-permute-start
  130.1 2.4 collective-permute-done
  133.2 1.9 collective-permute-start.1
  135.7 3.9 collective-permute-start
  139.7 2.4 collective-permute-done
  142.8 1.9 collective-permute-start.1
  145.3 3.9 collective-permute-start
  149.3 2.4 collective-permute-done
  152.5 1.9 collective-permute-start.1
  155.0 3.9 collective-permute-start
  158.9 2.4 collective-permute-done
  162.1 1.9 collective-permute-start.1
  164.6 3.9 collective-permute-start
  168.5 2.4 collective-permute-done
  171.7 1.9 collective-permute-start.1
  174.2 3.9 collective-permute-start
  178.1 2.4 collective-permute-done
  180.6 37.9 %while.57 = (s32[]{:T(128)}, f32[2,256]{1,0:T(2,128)S(1)}, f32[64,2,256]{2,0,1:T(8,128)S(1)}, pred[64,2]{1,0:T(8,128)(4,1)S(1)}, f32[64,2,256]{2,1,0:T(2,128)S(1...) while((s32[]{:T(128)}, f32[2,256]{1,0:T(2,128)S(1)}, f32[64,2,256]{2,0,1:T(8,128)S(1)}, ...), condition=%wide.region_13.14_spmd, body=%wide.region_11.13_spmd.sunk | while | flops 1574913 | bytes 282763 | solution.py:104
  218.5 35.2 %while.56 = (s32[]{:T(128)}, f32[2,256]{1,0:T(2,128)S(1)}, f32[64,2,256]{2,0,1:T(8,128)S(1)}, f32[64,2]{1,0:T(8,128)S(1)}, pred[64,2]{1,0:T(8,128)(4,1)S(1)}, /*...) while((s32[]{:T(128)}, f32[2,256]{1,0:T(2,128)S(1)}, ...), condition=%wide.region_10.11_spmd, body=%wide.region_8.10_spmd.sunk | while | flops 1574914 | bytes 282793 | solution.py:96
  254.2 3.4 scatter_custom_fusion
  257.6 20.5 %psum.15 = f32[2]{0:T(128)S(1)} all-reduce(f32[2]{0:T(128)S(1)} %reduce_sum.94), channel_id=1, replica_groups=mesh['tm'=8,'emit'=4] {'tm'}, use_global_device_ids=true, to_apply=%region_20.21 | all-reduce | flops 2 | bytes 16 | tf_op jit(solution)/shard_map/psum | solution.py:125
  279.3 100.1 %reduce-scatter.2.cloned.1.call-done = f32[128,256]{1,0:T(8,128)} async-done(((f32[4096,256]{1,0:T(8,128)}), f32[128,256]{1,0:T(8,128)}) %reduce-scatter.2.cloned.1.call-update) | async-done | bytes 131088 | tf_op jit(solution)/shard_map/reduce_scatter | solution.py:114
  379.4 0.9 reduce_sum.93
  380.3 63.2 %psum.14 = f32[256]{0:T(256)S(1)} all-reduce(f32[256]{0:T(256)S(1)} %reduce_sum.93), channel_id=1, replica_groups=mesh['tm'=8,'emit'=4] {'tm','emit'}, use_global_device_ids=true, to_apply=%region_18.19 | all-reduce | flops 256 | bytes 2048 | tf_op jit(solution)/shard_map/psum | solution.py:124
  443.4 1.6 multiply_divide_fusion
  (1109 shorter events, 120.8 us)
Async XLA Ops:
  7.2 33.1 %copy-start.1 = (f32[1024,256]{1,0:T(8,128)S(1)}, f32[1024,256]{1,0:T(8,128)}, u32[]{:S(2)}) copy-start(f32[1024,256]{1,0:T(8,128)} %param.17) | copy-start | bytes 3145732
  7.2 34.2 %copy-start.2 = (f32[256]{0:T(256)S(1)}, f32[256]{0:T(256)}, u32[]{:S(2)}) copy-start(f32[256]{0:T(256)} %param.15) | copy-start | bytes 3076
  7.2 372.2 %reduce-scatter.2.cloned.1.call-start = ((), (), s32[]{:S(2)}) async-start(), calls=%async_computation.1 | async-start | bytes 4325376 | tf_op jit(solution)/shard_map/reduce_scatter | solution.py:114
  7.2 14.5 %collective-permute-start.2 = (f32[1024,256]{1,0:T(8,128)}, f32[1024,256]{1,0:T(8,128)S(1)}, u32[]{:S(2)}, u32[]{:S(2)}) collective-permute-start(f32[1024,256]{1,0:T(8,128)} %param.17), channel_id=1, source_target_pairs={{0,1},{1,2},{2,3},{3,0},{4,5},{5,6},{6,7},{7,4},{8,9},{9,10},{10,1... | collective-permute-start | bytes 3145736 | tf_op jit(solution)/shard_map/ppermute | solution.py:46
  21.7 14.2 %collective-permute-start.3 = (f32[1024,256]{1,0:T(8,128)S(1)}, f32[1024,256]{1,0:T(8,128)S(1)}, u32[]{:S(2)}, u32[]{:S(2)}) collective-permute-start(f32[1024,256]{1,0:T(8,128)S(1)} %collective-permute-done.2), channel_id=1, source_target_pairs={{0,1},{1,2},{2,3},{3,0},{4,5},{5,6},{6,7},{7,4},{8,9},{9,10},{10,1... | collective-permute-start | bytes 3145736 | tf_op jit(solution)/shard_map/ppermute | solution.py:46
  35.9 14.3 %collective-permute-start.4 = (f32[1024,256]{1,0:T(8,128)S(1)}, f32[1024,256]{1,0:T(8,128)}, u32[]{:S(2)}, u32[]{:S(2)}) collective-permute-start(f32[1024,256]{1,0:T(8,128)S(1)} %collective-permute-done.3), channel_id=1, source_target_pairs={{0,1},{1,2},{2,3},{3,0},{4,5},{5,6},{6,7},{7,4},{8,9},{9,10},{10,1... | collective-permute-start | bytes 3145736 | tf_op jit(solution)/shard_map/ppermute | solution.py:46
  42.0 13.7 %copy-start = (f32[256,256]{1,0:T(8,128)S(1)}, f32[256,256]{1,0:T(8,128)}, u32[]{:S(2)}) copy-start(f32[256,256]{1,0:T(8,128)} %param.16) | copy-start | bytes 786436
  112.6 6.4 %collective-permute-start.1 = (f32[2,256]{1,0:T(2,128)S(1)}, f32[2,256]{1,0:T(2,128)S(1)}, u32[]{:S(2)}, u32[]{:S(2)}) collective-permute-start(f32[2,256]{1,0:T(2,128)S(1)} %bitcast_divide_fusion.5), channel_id=1, source_target_pairs={{4,0},{8,4},{12,8},{16,12},{20,16},{24,20},{28,24},{5,1},{9,5},{13... | collective-permute-start | bytes 6152 | tf_op jit(solution)/shard_map/while/body/eval_jaxpr/ppermute | solution.py:13
  116.5 6.4 %collective-permute-start = (f32[2,256]{1,0:T(2,128)S(1)}, f32[2,256]{1,0:T(2,128)S(1)}, u32[]{:S(2)}, u32[]{:S(2)}) collective-permute-start(f32[2,256]{1,0:T(2,128)S(1)} %bitcast_divide_fusion.4), channel_id=1, source_target_pairs={{0,4},{4,8},{8,12},{12,16},{16,20},{20,24},{24,28},{1,5},{5,9},{9,... | collective-permute-start | bytes 6152 | tf_op jit(solution)/shard_map/while/body/eval_jaxpr/ppermute | solution.py:13
  123.6 6.4 %collective-permute-start.1 = (f32[2,256]{1,0:T(2,128)S(1)}, f32[2,256]{1,0:T(2,128)S(1)}, u32[]{:S(2)}, u32[]{:S(2)}) collective-permute-start(f32[2,256]{1,0:T(2,128)S(1)} %bitcast_divide_fusion.5), channel_id=1, source_target_pairs={{4,0},{8,4},{12,8},{16,12},{20,16},{24,20},{28,24},{5,1},{9,5},{13... | collective-permute-start | bytes 6152 | tf_op jit(solution)/shard_map/while/body/eval_jaxpr/ppermute | solution.py:13
  126.1 6.4 %collective-permute-start = (f32[2,256]{1,0:T(2,128)S(1)}, f32[2,256]{1,0:T(2,128)S(1)}, u32[]{:S(2)}, u32[]{:S(2)}) collective-permute-start(f32[2,256]{1,0:T(2,128)S(1)} %bitcast_divide_fusion.4), channel_id=1, source_target_pairs={{0,4},{4,8},{8,12},{12,16},{16,20},{20,24},{24,28},{1,5},{5,9},{9,... | collective-permute-start | bytes 6152 | tf_op jit(solution)/shard_map/while/body/eval_jaxpr/ppermute | solution.py:13
  133.2 6.4 %collective-permute-start.1 = (f32[2,256]{1,0:T(2,128)S(1)}, f32[2,256]{1,0:T(2,128)S(1)}, u32[]{:S(2)}, u32[]{:S(2)}) collective-permute-start(f32[2,256]{1,0:T(2,128)S(1)} %bitcast_divide_fusion.5), channel_id=1, source_target_pairs={{4,0},{8,4},{12,8},{16,12},{20,16},{24,20},{28,24},{5,1},{9,5},{13... | collective-permute-start | bytes 6152 | tf_op jit(solution)/shard_map/while/body/eval_jaxpr/ppermute | solution.py:13
  135.7 6.4 %collective-permute-start = (f32[2,256]{1,0:T(2,128)S(1)}, f32[2,256]{1,0:T(2,128)S(1)}, u32[]{:S(2)}, u32[]{:S(2)}) collective-permute-start(f32[2,256]{1,0:T(2,128)S(1)} %bitcast_divide_fusion.4), channel_id=1, source_target_pairs={{0,4},{4,8},{8,12},{12,16},{16,20},{20,24},{24,28},{1,5},{5,9},{9,... | collective-permute-start | bytes 6152 | tf_op jit(solution)/shard_map/while/body/eval_jaxpr/ppermute | solution.py:13
  142.8 6.4 %collective-permute-start.1 = (f32[2,256]{1,0:T(2,128)S(1)}, f32[2,256]{1,0:T(2,128)S(1)}, u32[]{:S(2)}, u32[]{:S(2)}) collective-permute-start(f32[2,256]{1,0:T(2,128)S(1)} %bitcast_divide_fusion.5), channel_id=1, source_target_pairs={{4,0},{8,4},{12,8},{16,12},{20,16},{24,20},{28,24},{5,1},{9,5},{13... | collective-permute-start | bytes 6152 | tf_op jit(solution)/shard_map/while/body/eval_jaxpr/ppermute | solution.py:13
  145.3 6.4 %collective-permute-start = (f32[2,256]{1,0:T(2,128)S(1)}, f32[2,256]{1,0:T(2,128)S(1)}, u32[]{:S(2)}, u32[]{:S(2)}) collective-permute-start(f32[2,256]{1,0:T(2,128)S(1)} %bitcast_divide_fusion.4), channel_id=1, source_target_pairs={{0,4},{4,8},{8,12},{12,16},{16,20},{20,24},{24,28},{1,5},{5,9},{9,... | collective-permute-start | bytes 6152 | tf_op jit(solution)/shard_map/while/body/eval_jaxpr/ppermute | solution.py:13
  152.5 6.4 %collective-permute-start.1 = (f32[2,256]{1,0:T(2,128)S(1)}, f32[2,256]{1,0:T(2,128)S(1)}, u32[]{:S(2)}, u32[]{:S(2)}) collective-permute-start(f32[2,256]{1,0:T(2,128)S(1)} %bitcast_divide_fusion.5), channel_id=1, source_target_pairs={{4,0},{8,4},{12,8},{16,12},{20,16},{24,20},{28,24},{5,1},{9,5},{13... | collective-permute-start | bytes 6152 | tf_op jit(solution)/shard_map/while/body/eval_jaxpr/ppermute | solution.py:13
  155.0 6.4 %collective-permute-start = (f32[2,256]{1,0:T(2,128)S(1)}, f32[2,256]{1,0:T(2,128)S(1)}, u32[]{:S(2)}, u32[]{:S(2)}) collective-permute-start(f32[2,256]{1,0:T(2,128)S(1)} %bitcast_divide_fusion.4), channel_id=1, source_target_pairs={{0,4},{4,8},{8,12},{12,16},{16,20},{20,24},{24,28},{1,5},{5,9},{9,... | collective-permute-start | bytes 6152 | tf_op jit(solution)/shard_map/while/body/eval_jaxpr/ppermute | solution.py:13
  162.1 6.4 %collective-permute-start.1 = (f32[2,256]{1,0:T(2,128)S(1)}, f32[2,256]{1,0:T(2,128)S(1)}, u32[]{:S(2)}, u32[]{:S(2)}) collective-permute-start(f32[2,256]{1,0:T(2,128)S(1)} %bitcast_divide_fusion.5), channel_id=1, source_target_pairs={{4,0},{8,4},{12,8},{16,12},{20,16},{24,20},{28,24},{5,1},{9,5},{13... | collective-permute-start | bytes 6152 | tf_op jit(solution)/shard_map/while/body/eval_jaxpr/ppermute | solution.py:13
  164.6 6.4 %collective-permute-start = (f32[2,256]{1,0:T(2,128)S(1)}, f32[2,256]{1,0:T(2,128)S(1)}, u32[]{:S(2)}, u32[]{:S(2)}) collective-permute-start(f32[2,256]{1,0:T(2,128)S(1)} %bitcast_divide_fusion.4), channel_id=1, source_target_pairs={{0,4},{4,8},{8,12},{12,16},{16,20},{20,24},{24,28},{1,5},{5,9},{9,... | collective-permute-start | bytes 6152 | tf_op jit(solution)/shard_map/while/body/eval_jaxpr/ppermute | solution.py:13
  171.7 6.4 %collective-permute-start.1 = (f32[2,256]{1,0:T(2,128)S(1)}, f32[2,256]{1,0:T(2,128)S(1)}, u32[]{:S(2)}, u32[]{:S(2)}) collective-permute-start(f32[2,256]{1,0:T(2,128)S(1)} %bitcast_divide_fusion.5), channel_id=1, source_target_pairs={{4,0},{8,4},{12,8},{16,12},{20,16},{24,20},{28,24},{5,1},{9,5},{13... | collective-permute-start | bytes 6152 | tf_op jit(solution)/shard_map/while/body/eval_jaxpr/ppermute | solution.py:13
  174.2 6.4 %collective-permute-start = (f32[2,256]{1,0:T(2,128)S(1)}, f32[2,256]{1,0:T(2,128)S(1)}, u32[]{:S(2)}, u32[]{:S(2)}) collective-permute-start(f32[2,256]{1,0:T(2,128)S(1)} %bitcast_divide_fusion.4), channel_id=1, source_target_pairs={{0,4},{4,8},{8,12},{12,16},{16,20},{20,24},{24,28},{1,5},{5,9},{9,... | collective-permute-start | bytes 6152 | tf_op jit(solution)/shard_map/while/body/eval_jaxpr/ppermute | solution.py:13
  254.2 23.9 %copy-start.3 = (s32[2]{0:T(128)S(1)}, s32[2]{0:T(128)}, u32[]{:S(2)}) copy-start(s32[2]{0:T(128)} %param.14) | copy-start | bytes 28
Sparse Core Ops, SparseCore 0:
  257.7 121.5 reduce-scatter.1
